TPU v7x, 32 devices: a whole 2x2x4 slice. The times are simulated.
32 devices in a mesh: dp: 8 (over y, x, core), mp: 4 (over z).
Axes of the slice: x: 2, y: 2, z: 4, core: 2. Of those that a mesh axis runs over, the one named last changes fastest.
Arguments:
- pre: bfloat16 [1024, 12288], P('dp', 'mp'), may hold values from -32 to 32
- weight: float32 [6144, 12288], P('dp', 'mp'), may hold values from -0.0546875 to 0.0546875
- target: bfloat16 [6144, 1024], P('dp'), may hold values from -100 to 100
Outputs:
- update: float32 [6144, 12288], P('dp', 'mp')
All inputs are finite; a program needn't handle non-finite values.
Results may differ from a plain program's by a relative error of at most 0.0003.
The roundings to bfloat16 on the way count: a program that leaves them out, or rounds other values in their place, can miss the bound.
Values may be sent and summed in bfloat16 or wider, within the bound.
A program may use at most 64 MiB of HBM per device.

v0:
```python
import jax
import jax.numpy as jnp
from jax import lax
from jax.sharding import PartitionSpec as P

radius = 0.005
epsilon = 1e-06


def on_device(pre, weight, target):
    hidden = jax.nn.gelu(pre.astype(jnp.float32), approximate=False).astype(jnp.bfloat16)
    everyone = lax.all_gather(hidden, "dp", axis=0, tiled=True)
    entries = weight.shape[0] * weight.shape[1] * lax.axis_size("dp") * lax.axis_size("mp")

    def residual_of(matrix):
        partial_out = lax.dot_general(
            matrix, everyone, (((1,), (1,)), ((), ())), preferred_element_type=jnp.float32
        )
        summed = lax.psum(partial_out, "mp")
        result = (summed - target.astype(jnp.float32)).astype(jnp.bfloat16)
        return result

    resid = residual_of(weight.astype(jnp.bfloat16))
    ascent = jnp.dot(resid, everyone, preferred_element_type=jnp.float32)
    ascent_ms = lax.psum(jnp.sum(ascent * ascent), ("dp", "mp")) / entries
    perturbed = (weight + radius * jnp.tanh(ascent / jnp.sqrt(ascent_ms + epsilon))).astype(
        jnp.bfloat16
    )
    resid_two = residual_of(perturbed)
    descent = jnp.dot(resid_two, everyone, preferred_element_type=jnp.float32)
    descent_ms = lax.psum(jnp.sum(descent * descent), ("dp", "mp")) / entries
    return descent / jnp.sqrt(descent_ms + epsilon)


def solution(mesh):
    return jax.shard_map(
        on_device,
        mesh=mesh,
        in_specs=(P("dp", "mp"), P("dp", "mp"), P("dp", None)),
        out_specs=P("dp", "mp"),
        check_vma=False,
    )
```

profile of v0, /device:TPU:0, one launch (start us, length us, event | category | flops | bytes accessed | tf_op | source)
XLA Modules:
  0.0 443.9 jit_solution(3158897468256516652)
XLA Ops:
  6.5 0.0 all-gather.2.cloned.1.call-start
  6.5 5.1 %fusion.9 = bf16[128,3072]{1,0:T(8,128)(2,1)} fusion(bf16[128,3072]{1,0:T(8,128)(2,1)} %param.3), kind=kLoop, calls=%fused_computation.16 | loop fusion | flops 25952256 | bytes 1572864 | tf_op jit(solution)/shard_map/convert_element_type | solution.py:11
  11.7 0.0 all-gather.2.cloned.1.call-update
  11.7 0.0 all-reduce.3.cloned.1.call-start
  11.8 48.3 %all-gather.2.cloned.1.call-done = bf16[1024,3072]{1,0:T(8,128)(2,1)} async-done(((bf16[128,3072]{1,0:T(8,128)(2,1)}), bf16[1024,3072]{1,0:T(8,128)(2,1)}) %all-gather.2.cloned.1.call-update) | async-done | bytes 6291472 | tf_op jit(solution)/shard_map/all_gather | solution.py:12
  60.1 11.1 %fusion.5 = f32[768,1024]{1,0:T(8,128)} fusion(bf16[1024,3072]{1,0:T(8,128)(2,1)} %all-gather.2.cloned.1.call-done, f32[768,3072]{1,0:T(8,128)} %param.4), kind=kOutput, calls=%fused_computation.14 | convolution fusion | flops 4834197504 | bytes 18874368 | tf_op jit(solution)/shard_map/dot_general | solution.py:16
  71.2 0.0 copy-start
  71.2 0.0 all-reduce.3.cloned.1.call-update
  71.2 0.0 all-reduce.5.cloned.1.call-start
  71.2 121.2 %all-reduce.3.cloned.1.call-done = f32[768,1024]{1,0:T(8,128)} async-done(((f32[768,1024]{1,0:T(8,128)}), f32[768,1024]{1,0:T(8,128)}) %all-reduce.3.cloned.1.call-update) | async-done | bytes 3145744 | tf_op jit(solution)/shard_map/psum | solution.py:19
  192.4 0.0 copy-done
  192.4 11.1 %multiply_reduce_fusion.1 = (f32[]{:T(128)}, f32[768,3072]{1,0:T(8,128)}) fusion(bf16[1024,3072]{1,0:T(8,128)(2,1)} %all-gather.2.cloned.1.call-done, f32[768,1024]{1,0:T(8,128)} %all-reduce.3.cloned.1.call-done, bf16[768,1024]{1,0:T(8,128)(2,1)S(1)} %copy-done), kind=kOutput, calls=%fused_computation.2 | convolution fusion | flops 4838916096 | bytes 20447236 | tf_op jit(solution)/shard_map/dot_general | solution.py:24
  203.5 39.6 %psum.29 = f32[]{:T(128)} all-reduce(f32[]{:T(128)} %get-tuple-element.5), channel_id=1, replica_groups=mesh['dp'=8,'mp'=4] {'dp','mp'}, use_global_device_ids=true, to_apply=%region_2.0 | all-reduce | flops 1 | bytes 8 | tf_op jit(solution)/shard_map/psum | solution.py:25
  243.7 12.1 %fusion.2 = f32[768,1024]{1,0:T(8,128)} fusion(bf16[1024,3072]{1,0:T(8,128)(2,1)} %all-gather.2.cloned.1.call-done, f32[768,3072]{1,0:T(8,128)} %param.4, f32[768,3072]{1,0:T(8,128)} %get-tuple-element.6, f32[]{:T(128)S(6)} %sqrt.6), kind=kOutput, calls=%fused_computation.6 | convolution fusion | flops 4841275392 | bytes 28311556 | tf_op jit(solution)/shard_map/dot_general | solution.py:16
  255.8 0.0 all-reduce.5.cloned.1.call-update
  255.9 121.2 %all-reduce.5.cloned.1.call-done = f32[768,1024]{1,0:T(8,128)} async-done(((f32[768,1024]{1,0:T(8,128)}), f32[768,1024]{1,0:T(8,128)}) %all-reduce.5.cloned.1.call-update) | async-done | bytes 3145744 | tf_op jit(solution)/shard_map/psum | solution.py:19
  377.1 11.1 %multiply_reduce_fusion = (f32[]{:T(128)}, f32[768,3072]{1,0:T(8,128)}) fusion(bf16[1024,3072]{1,0:T(8,128)(2,1)} %all-gather.2.cloned.1.call-done, f32[768,1024]{1,0:T(8,128)} %all-reduce.5.cloned.1.call-done, bf16[768,1024]{1,0:T(8,128)(2,1)S(1)} %copy-done), kind=kOutput, calls=%fused_computation | convolution fusion | flops 4838916096 | bytes 20447236 | tf_op jit(solution)/shard_map/dot_general | solution.py:30
  388.2 39.4 %psum.31 = f32[]{:T(128)} all-reduce(f32[]{:T(128)} %get-tuple-element.7), channel_id=1, replica_groups=mesh['dp'=8,'mp'=4] {'dp','mp'}, use_global_device_ids=true, to_apply=%region_5.0 | all-reduce | flops 1 | bytes 8 | tf_op jit(solution)/shard_map/psum | solution.py:31
  428.3 9.0 %broadcast_divide_fusion = f32[768,3072]{1,0:T(8,128)} fusion(f32[768,3072]{1,0:T(8,128)} %get-tuple-element.8, f32[]{:T(128)S(6)} %sqrt.7), kind=kLoop, calls=%fused_computation.3 | loop fusion | flops 2359296 | bytes 18874372 | tf_op jit(solution)/shard_map/div | solution.py:32
Async XLA Ops:
  6.5 53.5 %all-gather.2.cloned.1.call-start = ((), (), s32[]{:S(2)}) async-start(), calls=%async_computation | async-start | bytes 7077888 | tf_op jit(solution)/shard_map/all_gather | solution.py:12
  11.7 180.7 %all-reduce.3.cloned.1.call-start = ((), (), s32[]{:S(2)}) async-start(), calls=%async_computation.1 | async-start | bytes 6291456 | tf_op jit(solution)/shard_map/psum | solution.py:19
  71.2 121.3 %copy-start = (bf16[768,1024]{1,0:T(8,128)(2,1)S(1)}, bf16[768,1024]{1,0:T(8,128)(2,1)}, u32[]{:S(2)}) copy-start(bf16[768,1024]{1,0:T(8,128)(2,1)} %param.5) | copy-start | bytes 4718596
  71.2 305.9 %all-reduce.5.cloned.1.call-start = ((), (), s32[]{:S(2)}) async-start(), calls=%async_computation.2 | async-start | bytes 6291456 | tf_op jit(solution)/shard_map/psum | solution.py:19
Sparse Core Ops, SparseCore 0:
  11.8 48.2 all-gather.1
  71.3 121.0 all-reduce.2
  256.0 121.0 all-reduce.4
where the time goes:
time: 444 us
  waiting for transfers between devices  291 us (66%)
  blocking collectives  79 us (18%)
  matrix products  45.4 us (10%)
  between operations  14.5 us (3%)
  other arithmetic  14.2 us (3%)
    psum x2, waiting for transfers between devices, residual_of(): summed = lax.psum(partial_out, 'mp')  242 us
    all_gather x1, waiting for transfers between devices, on_device(): everyone = lax.all_gather(hidden, 'dp', axis=0, tiled=True)  48.3 us
    psum x1, blocking collectives, on_device(): ascent_ms = lax.psum(jnp.sum(ascent * ascent), ('dp', 'mp')) / entries  39.6 us
    psum x1, blocking collectives, on_device(): descent_ms = lax.psum(jnp.sum(descent * descent), ('dp', 'mp')) / entries  39.4 us
    dot_general x2, matrix products, residual_of(): lax.dot_general(matrix, everyone, (((1,), (1,)), ((), ())), preferred_ele...  23.2 us
    dot_general x1, matrix products, on_device(): ascent = jnp.dot(resid, everyone, preferred_element_type=jnp.float32)  11.1 us
    dot_general x1, matrix products, on_device(): descent = jnp.dot(resid_two, everyone, preferred_element_type=jnp.float32)  11.1 us
    div x1, other arithmetic, on_device(): return descent / jnp.sqrt(descent_ms + epsilon)  9.05 us
  transfers between devices with their start and end apart: 3, of which 3 were waited for; matrix products, arithmetic and copies ran while one was open for 0% of the time, Pallas kernels for 0%

commit v1 on v0

--- a/solution.py
+++ b/solution.py
@@ -16,7 +16,7 @@
         partial_out = lax.dot_general(
             matrix, everyone, (((1,), (1,)), ((), ())), preferred_element_type=jnp.float32
         )
-        summed = lax.psum(partial_out, "mp")
+        summed = jnp.sum(lax.all_gather(partial_out, "mp"), axis=0)
         result = (summed - target.astype(jnp.float32)).astype(jnp.bfloat16)
         return result
 

time: 444 us -> 685 us (1.54)
  waiting for transfers between devices: 291 us -> 483 us
  other arithmetic: 14.2 us -> 41.9 us
  local copies, waits for them, and re-layouts: 0.01 us -> 21.4 us
    all_gather x0 -> x2, waiting for transfers between devices: none -> 435 us  [residual_of(): summed = jnp.sum(lax.all_gather(partial_out, 'mp'), axis=0)]
    psum x2 -> x0, waiting for transfers between devices: 242 us -> none  [residual_of(): summed = lax.psum(partial_out, 'mp')]
    reduce_sum x0 -> x2, other arithmetic: none -> 27.7 us  [residual_of(): summed = jnp.sum(lax.all_gather(partial_out, 'mp'), axis=0)]
    all_gather x0 -> x1, local copies, waits for them, and re-layouts: none -> 15.8 us  [residual_of(): summed = jnp.sum(lax.all_gather(partial_out, 'mp'), axis=0)]
where the time goes in v1:
time: 685 us
  waiting for transfers between devices  483 us (71%)
  blocking collectives  77.3 us (11%)
  matrix products  46.2 us (7%)
  other arithmetic  41.9 us (6%)
  local copies, waits for them, and re-layouts  21.4 us (3%)
  between operations  14.5 us (2%)
    all_gather x2, waiting for transfers between devices, residual_of(): summed = jnp.sum(lax.all_gather(partial_out, 'mp'), axis=0)  435 us
    all_gather x1, waiting for transfers between devices, on_device(): everyone = lax.all_gather(hidden, 'dp', axis=0, tiled=True)  48.3 us
    psum x1, blocking collectives, on_device(): ascent_ms = lax.psum(jnp.sum(ascent * ascent), ('dp', 'mp')) / entries  38.8 us
    psum x1, blocking collectives, on_device(): descent_ms = lax.psum(jnp.sum(descent * descent), ('dp', 'mp')) / entries  38.5 us
    reduce_sum x2, other arithmetic, residual_of(): summed = jnp.sum(lax.all_gather(partial_out, 'mp'), axis=0)  27.7 us
    dot_general x2, matrix products, residual_of(): lax.dot_general(matrix, everyone, (((1,), (1,)), ((), ())), preferred_ele...  23.1 us
    all_gather x1, local copies, waits for them, and re-layouts, residual_of(): summed = jnp.sum(lax.all_gather(partial_out, 'mp'), axis=0)  15.8 us
  transfers between devices with their start and end apart: 3, of which 3 were waited for; matrix products, arithmetic and copies ran while one was open for 0% of the time, Pallas kernels for 0%

profile of v1, /device:TPU:0, one launch (start us, length us, event | category | flops | bytes accessed | tf_op | source)
XLA Modules:
  0.0 684.5 jit_solution(12425069250434969560)
XLA Ops:
  6.5 0.0 all-gather.6.cloned.1.call-start
  6.5 5.1 fusion.9
  11.7 0.0 all-gather.6.cloned.1.call-update
  11.7 0.0 all-gather.8.cloned.1.call-start
  11.8 48.3 %all-gather.6.cloned.1.call-done = bf16[1024,3072]{1,0:T(8,128)(2,1)} async-done(((bf16[128,3072]{1,0:T(8,128)(2,1)}), bf16[1024,3072]{1,0:T(8,128)(2,1)}) %all-gather.6.cloned.1.call-update) | async-done | bytes 6291472 | tf_op jit(solution)/shard_map/all_gather | solution.py:12
  60.1 11.1 %fusion.5 = f32[768,1024]{0,1:T(8,128)} fusion(bf16[1024,3072]{1,0:T(8,128)(2,1)} %all-gather.6.cloned.1.call-done, f32[768,3072]{1,0:T(8,128)} %param.4), kind=kOutput, calls=%fused_computation.14 | convolution fusion | flops 4834197504 | bytes 18874368 | tf_op jit(solution)/shard_map/dot_general | solution.py:16
  71.2 0.0 copy-start
  71.2 0.0 all-gather.8.cloned.1.call-update
  71.2 0.0 all-gather.10.cloned.1.call-start
  71.2 1.3 copy-done
  72.6 0.7 copy.5
  73.3 216.3 %all-gather.8.cloned.1.call-done = f32[3072,1024]{0,1:T(8,128)} async-done(((f32[768,1024]{0,1:T(8,128)}), f32[3072,1024]{0,1:T(8,128)}) %all-gather.8.cloned.1.call-update) | async-done | bytes 12582928 | tf_op jit(solution)/shard_map/all_gather | solution.py:19
  289.6 15.8 %reshape = f32[4,768,1024]{1,0,2:T(4,128)} reshape(f32[3072,1024]{0,1:T(8,128)} %all-gather.8.cloned.1.call-done) | data formatting | bytes 25165824 | tf_op jit(solution)/shard_map/all_gather | solution.py:19
  305.3 19.6 %reduce_sum.36 = f32[768,1024]{0,1:T(8,128)} reduce(f32[4,768,1024]{1,0,2:T(4,128)} %reshape, f32[]{:T(128)} %constant.11.clone.1), dimensions={0}, to_apply=%region_0.0 | reduce | flops 2359296 | bytes 15728644 | tf_op jit(solution)/shard_map/reduce_sum | solution.py:19
  324.9 11.6 %multiply_reduce_fusion.1 = (f32[]{:T(128)}, f32[768,3072]{1,0:T(8,128)}) fusion(bf16[1024,3072]{1,0:T(8,128)(2,1)} %all-gather.6.cloned.1.call-done, f32[768,1024]{0,1:T(8,128)} %reduce_sum.36, bf16[768,1024]{0,1:T(8,128)(2,1)S(1)} %copy.5), kind=kOutput, calls=%fused_computation.2 | convolution fusion | flops 4838916096 | bytes 20447236 | tf_op jit(solution)/shard_map/dot_general | solution.py:24
  336.5 38.8 %psum.14 = f32[]{:T(128)} all-reduce(f32[]{:T(128)} %get-tuple-element.5), channel_id=1, replica_groups=mesh['dp'=8,'mp'=4] {'dp','mp'}, use_global_device_ids=true, to_apply=%region_2.0 | all-reduce | flops 1 | bytes 8 | tf_op jit(solution)/shard_map/psum | solution.py:25
  376.0 12.0 %fusion.2 = f32[768,1024]{1,0:T(8,128)} fusion(bf16[1024,3072]{1,0:T(8,128)(2,1)} %all-gather.6.cloned.1.call-done, f32[768,3072]{1,0:T(8,128)} %param.4, f32[768,3072]{1,0:T(8,128)} %get-tuple-element.6, f32[]{:T(128)S(6)} %sqrt.6), kind=kOutput, calls=%fused_computation.6 | convolution fusion | flops 4841275392 | bytes 28311556 | tf_op jit(solution)/shard_map/dot_general | solution.py:16
  388.0 0.0 all-gather.10.cloned.1.call-update
  388.0 218.4 %all-gather.10.cloned.1.call-done = f32[3072,1024]{1,0:T(8,128)} async-done(((f32[768,1024]{1,0:T(8,128)}), f32[3072,1024]{1,0:T(8,128)}) %all-gather.10.cloned.1.call-update) | async-done | bytes 12582928 | tf_op jit(solution)/shard_map/all_gather | solution.py:19
  606.5 8.1 %reduce_sum.38 = f32[768,1024]{1,0:T(8,128)} reduce(f32[4,768,1024]{2,1,0:T(8,128)} %bitcast.9, f32[]{:T(128)} %constant.11.clone.1), dimensions={0}, to_apply=%region_3.0 | reduce | flops 2359296 | bytes 15728644 | tf_op jit(solution)/shard_map/reduce_sum | solution.py:19
  614.6 3.5 copy.6
  618.1 11.5 %multiply_reduce_fusion = (f32[]{:T(128)}, f32[768,3072]{1,0:T(8,128)}) fusion(bf16[1024,3072]{1,0:T(8,128)(2,1)} %all-gather.6.cloned.1.call-done, f32[768,1024]{0,1:T(8,128)} %copy.6, bf16[768,1024]{0,1:T(8,128)(2,1)S(1)} %copy.5), kind=kOutput, calls=%fused_computation | convolution fusion | flops 4838916096 | bytes 20447236 | tf_op jit(solution)/shard_map/dot_general | solution.py:30
  629.7 38.5 %psum.15 = f32[]{:T(128)} all-reduce(f32[]{:T(128)} %get-tuple-element.7), channel_id=1, replica_groups=mesh['dp'=8,'mp'=4] {'dp','mp'}, use_global_device_ids=true, to_apply=%region_5.0 | all-reduce | flops 1 | bytes 8 | tf_op jit(solution)/shard_map/psum | solution.py:31
  668.9 9.0 %broadcast_divide_fusion = f32[768,3072]{1,0:T(8,128)} fusion(f32[768,3072]{1,0:T(8,128)} %get-tuple-element.8, f32[]{:T(128)S(6)} %sqrt.7), kind=kLoop, calls=%fused_computation.3 | loop fusion | flops 2359296 | bytes 18874372 | tf_op jit(solution)/shard_map/div | solution.py:32
Async XLA Ops:
  6.5 53.5 %all-gather.6.cloned.1.call-start = ((), (), s32[]{:S(2)}) async-start(), calls=%async_computation | async-start | bytes 7077888 | tf_op jit(solution)/shard_map/all_gather | solution.py:12
  11.7 277.8 %all-gather.8.cloned.1.call-start = ((), (), s32[]{:S(2)}) async-start(), calls=%async_computation.1 | async-start | bytes 15728640 | tf_op jit(solution)/shard_map/all_gather | solution.py:19
  71.2 1.4 copy-start
  71.2 535.3 %all-gather.10.cloned.1.call-start = ((), (), s32[]{:S(2)}) async-start(), calls=%async_computation.2 | async-start | bytes 15728640 | tf_op jit(solution)/shard_map/all_gather | solution.py:19
Sparse Core Ops, SparseCore 0:
  11.8 48.2 all-gather.5
  71.3 218.1 all-gather.7
  388.2 218.2 all-gather.9
